TPU v7x, 32 devices: a whole 2x2x4 slice. The times are simulated.
32 devices in a mesh: dp: 8 (over z, y), section: 2 (over core), tensor: 2 (over x).
Axes of the slice: x: 2, y: 2, z: 4, core: 2. Of those that a mesh axis runs over, the one named last changes fastest.
Arguments:
- tokens: bfloat16 [128, 32, 1024], P('dp'), may hold values from -6 to 6
- counts: int32 [128], replicated, may hold values from 8 to 32, as said below
- assign: int32 [128], replicated, may hold values from 0 to 127, as said below
- qkv_weight: bfloat16 [2, 1024, 3, 1024], P('section', 'dp', None, 'tensor'), may hold values from -0.9375 to 0.9375
- out_weight: bfloat16 [2, 1024, 1024], P('section', 'dp'), may hold values from -0.1875 to 0.1875
- up_weight: bfloat16 [2, 1024, 4096], P('section', 'dp', 'tensor'), may hold values from -0.1875 to 0.1875
- up_bias: bfloat16 [2, 4096], P('section', 'tensor'), may hold values from -3 to 3
- down_weight: bfloat16 [2, 4096, 1024], P('section', 'tensor', 'dp'), may hold values from -0.09375 to 0.09375
- attn_gain: bfloat16 [2, 1024], P('section'), may hold values from 0.25 to 1.75
- mlp_gain: bfloat16 [2, 1024], P('section'), may hold values from 0.25 to 1.75
- final_gain: bfloat16 [1024], replicated, may hold values from 0.25 to 1.75
Outputs:
- encoded: bfloat16 [128, 32, 1024], P('dp', 'section', 'tensor')
Inputs may be any that keep to these rules, and one draw needn't show every extreme that they name: `counts`: every count is at least 8, and in every draw some image has all 32 slots live. assign is a permutation of the images. Slot j belongs to data group j // 16, so every data group receives 16 images; within one data group's slots the images stand in increasing order. Images of data group g are tokens rows g * 16 to (g + 1) * 16 - 1. No data group hands more than 2 images to one data group (itself included), and in every draw some pair of data groups exchanges exactly 2. Every data group receives some image from the data group half the axis away.
All inputs are finite; a program needn't handle non-finite values.
Results may differ from a plain program's by a relative error of at most 0.024.
The roundings to bfloat16 on the way count: a program that leaves them out, or rounds other values in their place, can miss the bound.
Values may be sent and summed in bfloat16 or wider, within the bound.
A program may use at most 128 MiB of HBM per device.

v0:
```python
import jax
import jax.numpy as jnp
from jax import lax
from jax.sharding import PartitionSpec as P

MICRO = 4
HEAD_DIM = 64
epsilon = 1e-06


def passed_along(value, axis, by):
    size = lax.axis_size(axis)
    return lax.ppermute(value, axis, [(i, (i + by) % size) for i in range(size)])


def broadcast(value, axis, root):
    mine = lax.axis_index(axis) == root
    return lax.psum(jnp.where(mine, value, jnp.zeros_like(value)), axis)


def layer_norm(values, gain_vector):
    average = jnp.mean(values, axis=-1, keepdims=True)
    centred = values - average
    spread = jnp.mean(centred * centred, axis=-1, keepdims=True)
    return centred * lax.rsqrt(spread + epsilon) * gain_vector.astype(jnp.float32)


def attend(normed, w_merged, live_count, head_dim):
    row_count = normed.shape[0]
    merged = jnp.dot(
        normed, w_merged.reshape(w_merged.shape[0], -1), preferred_element_type=jnp.float32
    )
    merged = merged.reshape(row_count, 3, -1, head_dim)
    scores = jnp.einsum(
        "qhd,khd->hqk", merged[:, 0], merged[:, 1], precision=lax.Precision.HIGHEST
    ) * head_dim ** (-0.5)
    visible = jnp.arange(row_count) < live_count
    scores = jnp.where(visible[None, None, :], scores, -1e30)
    weights = jax.nn.softmax(scores, axis=-1)
    mixed = jnp.einsum("hqk,khd->qhd", weights, merged[:, 2], precision=lax.Precision.HIGHEST)
    return mixed.reshape(row_count, -1).astype(jnp.bfloat16)


def local(
    tokens,
    counts,
    assign,
    qkv_weight,
    out_weight,
    up_weight,
    up_bias,
    down_weight,
    attn_gain,
    mlp_gain,
    final_gain,
):
    groups = lax.axis_size("dp")
    sections = lax.axis_size("section")
    tensor_ranks = lax.axis_size("tensor")
    images_dev, block_rows, model_width = tokens.shape
    quarter = model_width // tensor_ranks
    capacity = (images_dev + groups - 1) // groups
    total_images = assign.shape[0]
    batch_images = MICRO
    batch_count = images_dev // batch_images
    my_group = lax.axis_index("dp")
    my_section = lax.axis_index("section")
    tensor_index = lax.axis_index("tensor")
    numbers = jnp.arange(total_images, dtype=jnp.int32)
    matches = (assign[:, None] == numbers[None, :]).astype(jnp.int32)
    slot_of = jnp.sum(matches * numbers[:, None], axis=0)
    target = slot_of // images_dev
    source_group = numbers // images_dev
    earlier = (
        (source_group[:, None] == source_group[None, :])
        & (target[:, None] == target[None, :])
        & (numbers[None, :] < numbers[:, None])
    )
    rank_all = jnp.sum(earlier.astype(jnp.int32), axis=1)
    send_slot = lax.dynamic_slice_in_dim(
        target * capacity + rank_all, my_group * images_dev, images_dev
    )
    buffer_slots = jnp.arange(groups * capacity, dtype=jnp.int32)
    selector = (buffer_slots[:, None] == send_slot[None, :]).astype(jnp.bfloat16)
    outgoing = jnp.einsum(
        "sl,lbd->sbd", selector, tokens, preferred_element_type=jnp.float32
    ).astype(jnp.bfloat16)
    received = lax.all_to_all(outgoing, "dp", split_axis=0, concat_axis=0, tiled=True)
    my_images = lax.dynamic_slice_in_dim(assign, my_group * images_dev, images_dev)
    chosen = (my_images[:, None] == numbers[None, :]).astype(jnp.int32)
    receive_slot = jnp.sum(chosen * (source_group * capacity + rank_all)[None, :], axis=1)
    live_counts = jnp.sum(chosen * counts[None, :], axis=1)
    picker = (buffer_slots[None, :] == receive_slot[:, None]).astype(jnp.bfloat16)
    arrived = jnp.einsum(
        "js,sbd->jbd", picker, received, preferred_element_type=jnp.float32
    ).astype(jnp.bfloat16)
    arrived_batches = arrived.reshape(batch_count, batch_images, block_rows, model_width)
    live_batches = live_counts.reshape(batch_count, batch_images)
    qkv_full, out_full, up_full, down_full = (
        lax.all_gather(qkv_weight, "dp", axis=1, tiled=True),
        lax.all_gather(out_weight, "dp", axis=1, tiled=True),
        lax.all_gather(up_weight, "dp", axis=1, tiled=True),
        lax.all_gather(down_weight, "dp", axis=2, tiled=True),
    )
    qkv_full = qkv_full[0]
    out_full = out_full[0]
    up_full = up_full[0]
    down_full = down_full[0]
    bias_row = up_bias[0].astype(jnp.float32)
    gain_attn = attn_gain[0]
    gain_mlp = mlp_gain[0]
    row_numbers = jnp.arange(block_rows)
    flat_rows = batch_images * block_rows

    def advance(step_index, state):
        carried, stored = state
        current = lax.all_gather(carried, "tensor", axis=2, tiled=True)
        done_index = step_index - sections
        finishing = (my_section == 0) & (done_index >= 0)
        done_slot = jnp.clip(done_index, 0, batch_count - 1)
        finished_rows = row_numbers[None, :, None] < live_batches[done_slot][:, None, None]
        finished = jnp.where(
            finished_rows, layer_norm(current.astype(jnp.float32), final_gain), 0.0
        ).astype(jnp.bfloat16)
        stored = jnp.where(
            finishing, lax.dynamic_update_index_in_dim(stored, finished, done_slot, 0), stored
        )
        micro_index = step_index - my_section
        active = (micro_index >= 0) & (micro_index < batch_count)
        slot_index = jnp.clip(micro_index, 0, batch_count - 1)
        injected = lax.dynamic_index_in_dim(
            arrived_batches, jnp.clip(step_index, 0, batch_count - 1), 0, keepdims=False
        )
        incoming = jnp.where(my_section == 0, injected, current)
        live_now = live_batches[slot_index]

        def attention_part():
            normed = layer_norm(incoming.astype(jnp.float32), gain_attn).astype(jnp.bfloat16)
            return jax.vmap(
                lambda image_rows, live_count: attend(image_rows, qkv_full, live_count, HEAD_DIM)
            )(normed, live_now)

        def attention_spare():
            return jnp.zeros((batch_images, block_rows, quarter), jnp.bfloat16)

        head_out = lax.cond(active, attention_part, attention_spare)
        joined = lax.all_gather(head_out, "tensor", axis=2, tiled=True)

        def mlp_part():
            middle = incoming.reshape(flat_rows, model_width).astype(jnp.float32) + jnp.dot(
                joined.reshape(flat_rows, model_width), out_full, preferred_element_type=jnp.float32
            )
            normed_mlp = layer_norm(middle, gain_mlp).astype(jnp.bfloat16)
            hidden = jax.nn.gelu(
                jnp.dot(normed_mlp, up_full, preferred_element_type=jnp.float32) + bias_row,
                approximate=False,
            ).astype(jnp.bfloat16)
            return (middle, jnp.dot(hidden, down_full, preferred_element_type=jnp.float32))

        def mlp_spare():
            empty = jnp.zeros((flat_rows, model_width), jnp.float32)
            return (empty, empty)

        middle, partial_value = lax.cond(active, mlp_part, mlp_spare)
        shares = lax.psum_scatter(
            partial_value.astype(jnp.bfloat16), "tensor", scatter_dimension=1, tiled=True
        ).astype(jnp.float32)
        own_share = lax.dynamic_slice_in_dim(middle, tensor_index * quarter, quarter, 1)
        updated = (
            (own_share + shares).astype(jnp.bfloat16).reshape(batch_images, block_rows, quarter)
        )
        carried = passed_along(updated, "section", 1)
        return (carried, stored)

    initial = (
        jnp.zeros((batch_images, block_rows, quarter), jnp.bfloat16),
        jnp.zeros((batch_count, batch_images, block_rows, model_width), jnp.bfloat16),
    )
    carried, stored = lax.fori_loop(0, batch_count + sections, advance, initial)
    stored = stored.reshape(images_dev, block_rows, model_width)
    my_piece = lax.dynamic_slice_in_dim(stored, tensor_index * quarter, quarter, 2)
    spread = broadcast(my_piece, "section", 0)
    section_rows = block_rows // sections
    return lax.dynamic_slice_in_dim(spread, my_section * section_rows, section_rows, 1)


def solution(mesh):
    in_specs = (
        P("dp", None, None),
        P(),
        P(),
        P("section", "dp", None, "tensor"),
        P("section", "dp", None),
        P("section", "dp", "tensor"),
        P("section", "tensor"),
        P("section", "tensor", "dp"),
        P("section", None),
        P("section", None),
        P(),
    )
    out_specs = P("dp", "section", "tensor")
    return jax.shard_map(local, mesh=mesh, in_specs=in_specs, out_specs=out_specs, check_vma=False)
```

profile of v0, /device:TPU:0, one launch (start us, length us, event | category | flops | bytes accessed | tf_op | source)
XLA Modules:
  0.0 576.1 jit_solution(2311422766453699122)
XLA Ops:
  7.3 1.9 copy.31
  14.1 7.3 %all-to-all-start = ((bf16[16,32,1024]{2,1,0:T(8,128)(2,1)}), bf16[16,32,1024]{2,1,0:T(8,128)(2,1)S(1)}, u32[]{:S(2)}, u32[]{:S(2)}) async-start(bf16[16,32,1024]{2,1,0:T(8,128)(2,1)} %copy.29), calls=%async_computation.1 | async-start | bytes 2097152 | tf_op jit(solution)/shard_map/all_to_all | solution.py:88
  21.8 36.7 %all-to-all-done = bf16[16,32,1024]{2,1,0:T(8,128)(2,1)S(1)} async-done(((bf16[16,32,1024]{2,1,0:T(8,128)(2,1)}), bf16[16,32,1024]{2,1,0:T(8,128)(2,1)S(1)}, u32[]{:S(2)}, u32[]{:S(2)}) %all-to-all-start) | async-done | bytes 1048608 | tf_op jit(solution)/shard_map/all_to_all | solution.py:88
  60.9 12.2 %all-gather.7.cloned.1.call-done = bf16[1,1024,1024]{2,1,0:T(8,128)(2,1)} async-done(((bf16[1,128,1024]{2,1,0:T(8,128)(2,1)}), bf16[1,1024,1024]{2,1,0:T(8,128)(2,1)}) %all-gather.7.cloned.1.call-update) | async-done | bytes 2097168 | tf_op jit(solution)/shard_map/all_gather | solution.py:101
  73.1 63.3 %all-gather.5.cloned.1.call-done = bf16[1,1024,3,512]{1,3,2,0:T(8,128)(2,1)} async-done(((bf16[1,128,3,512]{1,3,2,0:T(8,128)(2,1)}), bf16[1,1024,3,512]{1,3,2,0:T(8,128)(2,1)}) %all-gather.5.cloned.1.call-update) | async-done | bytes 3145744 | tf_op jit(solution)/shard_map/all_gather | solution.py:100
  136.4 73.2 %all-gather.9.cloned.1.call-done = bf16[1,1024,2048]{2,1,0:T(8,128)(2,1)} async-done(((bf16[1,128,2048]{2,1,0:T(8,128)(2,1)}), bf16[1,1024,2048]{2,1,0:T(8,128)(2,1)}) %all-gather.9.cloned.1.call-update) | async-done | bytes 4194320 | tf_op jit(solution)/shard_map/all_gather | solution.py:102
  209.5 75.1 %all-gather.11.cloned.1.call-done = bf16[1,2048,1024]{2,1,0:T(8,128)(2,1)} async-done(((bf16[1,2048,128]{2,1,0:T(8,128)(2,1)}), bf16[1,2048,1024]{2,1,0:T(8,128)(2,1)}) %all-gather.11.cloned.1.call-update) | async-done | bytes 4194320 | tf_op jit(solution)/shard_map/all_gather | solution.py:103
  285.7 260.2 %while.18 = (s32[]{:T(128)}, bf16[4,32,512]{2,1,0:T(8,128)(2,1)S(1)}, bf16[4,4,32,1024]{3,2,1,0:T(8,128)(2,1)}, s32[]{:T(128)}, pred[]{:T(512)}, /*index=5*/bf16...) while((s32[]{:T(128)}, ...), condition=%wide.region_18.19_spmd.clone, body=%wide.region_4.18_spmd.clone.sunk | while | flops 1817675392 | bytes 26838016 | solution.py:179
  285.8 5.6 all_gather.40
  292.4 6.5 %conditional.6 = (bf16[4,32,512]{2,1,0:T(8,128)(2,1)S(1)}) conditional(s32[]{:T(128)} %convert_element_type.220, () %tuple.73, (bf16[4,32,1024]{2,1,0:T(8,128)(2,1)S(1)}, bf16[1024]{0:T(1024)(128)(2,1)S(1)}, bf16[1,1024,3,512]{1,3,2,0:T(8,128)(2,1)}, s32[]{:T(128)}, s32[4,4]{1,0:T(4,128)S(1)}) %tuple.74), branch_computations={%region_5.5_spmd, %region_6.10_spmd} | conditional | flops 454720768 | bytes 7793876 | solution.py:146
  292.8 3.6 fusion.12
  299.0 5.6 all_gather.41
  304.6 11.4 %conditional.7 = (f32[128,1024]{1,0:T(8,128)}, f32[128,1024]{1,0:T(8,128)S(1)}) conditional(s32[]{:T(128)} %convert_element_type.220, () %tuple.72, (bf16[4,32,1024]{2,1,0:T(8,128)(2,1)S(1)}, bf16[4,32,1024]{2,1,0:T(8,128)(2,1)S(1)}, bf16[1024,1024]{1,0:T(8,128)(2,1)}, bf16[1024]{0:T(1024)(128)(2,1)S(1)}, bf16[1024,2048]{1,0:T(8,128)(2,1)}, ...), branch_computations={%region_11.11_spmd, %region_12.14_spmd} | conditional | flops 1360790656 | bytes 13130256 | solution.py:164
  304.6 2.8 fusion.117
  308.7 7.3 %fusion.29 = f32[128,1024]{1,0:T(8,128)S(1)} fusion(bf16[2048,1024]{1,0:T(8,128)(2,1)} %get-tuple-element.436, bf16[1024,2048]{1,0:T(8,128)(2,1)} %get-tuple-element.434, f32[2048]{0:T(1024)S(1)} %get-tuple-element.435, f32[128,1024]{1,0:T(8,128)} %get-tuple-element.704, f32[1024]{0:T(1024)S(1)} %convert_element_type.116, f32[128]{0:T(128)S(1)} %add_rsqrt_fusion.1, ...), kind=kOutput, calls=%fused_computation.50 | convolution fusion | flops 1091567616 | bytes 9450496 | tf_op jit(solution)/shard_map/while/body/eval_jaxpr/cond/branch_1_fun/dot_general | solution.py:158
  317.3 9.9 %reduce-scatter.2.cloned.1.call-done = bf16[128,512]{1,0:T(8,128)(2,1)} async-done(((bf16[128,1024]{1,0:T(8,128)(2,1)}), bf16[128,512]{1,0:T(8,128)(2,1)}) %reduce-scatter.2.cloned.1.call-update) | async-done | bytes 131088 | tf_op jit(solution)/shard_map/while/body/eval_jaxpr/reduce_scatter | solution.py:165
  330.3 6.5 %all_gather.40 = bf16[4,32,1024]{2,1,0:T(8,128)(2,1)S(1)} all-gather(bf16[4,32,512]{2,1,0:T(8,128)(2,1)S(1)} %get-tuple-element.728), channel_id=1, replica_groups=mesh['dp'=8,'section'=2,'tensor'=2] {'tensor'}, dimensions={2}, use_global_device_ids=true | all-gather | bytes 393216 | tf_op jit(solution)/shard_map/while/body/eval_jaxpr/all_gather | solution.py:117
  337.8 6.5 %conditional.6 = (bf16[4,32,512]{2,1,0:T(8,128)(2,1)S(1)}) conditional(s32[]{:T(128)} %convert_element_type.220, () %tuple.73, (bf16[4,32,1024]{2,1,0:T(8,128)(2,1)S(1)}, bf16[1024]{0:T(1024)(128)(2,1)S(1)}, bf16[1,1024,3,512]{1,3,2,0:T(8,128)(2,1)}, s32[]{:T(128)}, s32[4,4]{1,0:T(4,128)S(1)}) %tuple.74), branch_computations={%region_5.5_spmd, %region_6.10_spmd} | conditional | flops 454720768 | bytes 7793876 | solution.py:146
  338.2 3.6 fusion.12
  344.3 5.7 all_gather.41
  350.0 11.4 %conditional.7 = (f32[128,1024]{1,0:T(8,128)}, f32[128,1024]{1,0:T(8,128)S(1)}) conditional(s32[]{:T(128)} %convert_element_type.220, () %tuple.72, (bf16[4,32,1024]{2,1,0:T(8,128)(2,1)S(1)}, bf16[4,32,1024]{2,1,0:T(8,128)(2,1)S(1)}, bf16[1024,1024]{1,0:T(8,128)(2,1)}, bf16[1024]{0:T(1024)(128)(2,1)S(1)}, bf16[1024,2048]{1,0:T(8,128)(2,1)}, ...), branch_computations={%region_11.11_spmd, %region_12.14_spmd} | conditional | flops 1360790656 | bytes 13130256 | solution.py:164
  350.0 2.8 fusion.117
  354.1 7.3 %fusion.29 = f32[128,1024]{1,0:T(8,128)S(1)} fusion(bf16[2048,1024]{1,0:T(8,128)(2,1)} %get-tuple-element.436, bf16[1024,2048]{1,0:T(8,128)(2,1)} %get-tuple-element.434, f32[2048]{0:T(1024)S(1)} %get-tuple-element.435, f32[128,1024]{1,0:T(8,128)} %get-tuple-element.704, f32[1024]{0:T(1024)S(1)} %convert_element_type.116, f32[128]{0:T(128)S(1)} %add_rsqrt_fusion.1, ...), kind=kOutput, calls=%fused_computation.50 | convolution fusion | flops 1091567616 | bytes 9450496 | tf_op jit(solution)/shard_map/while/body/eval_jaxpr/cond/branch_1_fun/dot_general | solution.py:158
  362.6 11.5 %reduce-scatter.2.cloned.1.call-done = bf16[128,512]{1,0:T(8,128)(2,1)} async-done(((bf16[128,1024]{1,0:T(8,128)(2,1)}), bf16[128,512]{1,0:T(8,128)(2,1)}) %reduce-scatter.2.cloned.1.call-update) | async-done | bytes 131088 | tf_op jit(solution)/shard_map/while/body/eval_jaxpr/reduce_scatter | solution.py:165
  377.2 6.5 %all_gather.40 = bf16[4,32,1024]{2,1,0:T(8,128)(2,1)S(1)} all-gather(bf16[4,32,512]{2,1,0:T(8,128)(2,1)S(1)} %get-tuple-element.728), channel_id=1, replica_groups=mesh['dp'=8,'section'=2,'tensor'=2] {'tensor'}, dimensions={2}, use_global_device_ids=true | all-gather | bytes 393216 | tf_op jit(solution)/shard_map/while/body/eval_jaxpr/all_gather | solution.py:117
  384.7 6.5 %conditional.6 = (bf16[4,32,512]{2,1,0:T(8,128)(2,1)S(1)}) conditional(s32[]{:T(128)} %convert_element_type.220, () %tuple.73, (bf16[4,32,1024]{2,1,0:T(8,128)(2,1)S(1)}, bf16[1024]{0:T(1024)(128)(2,1)S(1)}, bf16[1,1024,3,512]{1,3,2,0:T(8,128)(2,1)}, s32[]{:T(128)}, s32[4,4]{1,0:T(4,128)S(1)}) %tuple.74), branch_computations={%region_5.5_spmd, %region_6.10_spmd} | conditional | flops 454720768 | bytes 7793876 | solution.py:146
  385.1 3.6 fusion.12
  391.2 5.7 all_gather.41
  396.9 11.4 %conditional.7 = (f32[128,1024]{1,0:T(8,128)}, f32[128,1024]{1,0:T(8,128)S(1)}) conditional(s32[]{:T(128)} %convert_element_type.220, () %tuple.72, (bf16[4,32,1024]{2,1,0:T(8,128)(2,1)S(1)}, bf16[4,32,1024]{2,1,0:T(8,128)(2,1)S(1)}, bf16[1024,1024]{1,0:T(8,128)(2,1)}, bf16[1024]{0:T(1024)(128)(2,1)S(1)}, bf16[1024,2048]{1,0:T(8,128)(2,1)}, ...), branch_computations={%region_11.11_spmd, %region_12.14_spmd} | conditional | flops 1360790656 | bytes 13130256 | solution.py:164
  396.9 2.8 fusion.117
  401.0 7.3 %fusion.29 = f32[128,1024]{1,0:T(8,128)S(1)} fusion(bf16[2048,1024]{1,0:T(8,128)(2,1)} %get-tuple-element.436, bf16[1024,2048]{1,0:T(8,128)(2,1)} %get-tuple-element.434, f32[2048]{0:T(1024)S(1)} %get-tuple-element.435, f32[128,1024]{1,0:T(8,128)} %get-tuple-element.704, f32[1024]{0:T(1024)S(1)} %convert_element_type.116, f32[128]{0:T(128)S(1)} %add_rsqrt_fusion.1, ...), kind=kOutput, calls=%fused_computation.50 | convolution fusion | flops 1091567616 | bytes 9450496 | tf_op jit(solution)/shard_map/while/body/eval_jaxpr/cond/branch_1_fun/dot_general | solution.py:158
  409.6 11.5 %reduce-scatter.2.cloned.1.call-done = bf16[128,512]{1,0:T(8,128)(2,1)} async-done(((bf16[128,1024]{1,0:T(8,128)(2,1)}), bf16[128,512]{1,0:T(8,128)(2,1)}) %reduce-scatter.2.cloned.1.call-update) | async-done | bytes 131088 | tf_op jit(solution)/shard_map/while/body/eval_jaxpr/reduce_scatter | solution.py:165
  424.1 6.5 %all_gather.40 = bf16[4,32,1024]{2,1,0:T(8,128)(2,1)S(1)} all-gather(bf16[4,32,512]{2,1,0:T(8,128)(2,1)S(1)} %get-tuple-element.728), channel_id=1, replica_groups=mesh['dp'=8,'section'=2,'tensor'=2] {'tensor'}, dimensions={2}, use_global_device_ids=true | all-gather | bytes 393216 | tf_op jit(solution)/shard_map/while/body/eval_jaxpr/all_gather | solution.py:117
  431.7 6.5 %conditional.6 = (bf16[4,32,512]{2,1,0:T(8,128)(2,1)S(1)}) conditional(s32[]{:T(128)} %convert_element_type.220, () %tuple.73, (bf16[4,32,1024]{2,1,0:T(8,128)(2,1)S(1)}, bf16[1024]{0:T(1024)(128)(2,1)S(1)}, bf16[1,1024,3,512]{1,3,2,0:T(8,128)(2,1)}, s32[]{:T(128)}, s32[4,4]{1,0:T(4,128)S(1)}) %tuple.74), branch_computations={%region_5.5_spmd, %region_6.10_spmd} | conditional | flops 454720768 | bytes 7793876 | solution.py:146
  432.0 3.6 fusion.12
  438.2 5.7 all_gather.41
  443.9 11.4 %conditional.7 = (f32[128,1024]{1,0:T(8,128)}, f32[128,1024]{1,0:T(8,128)S(1)}) conditional(s32[]{:T(128)} %convert_element_type.220, () %tuple.72, (bf16[4,32,1024]{2,1,0:T(8,128)(2,1)S(1)}, bf16[4,32,1024]{2,1,0:T(8,128)(2,1)S(1)}, bf16[1024,1024]{1,0:T(8,128)(2,1)}, bf16[1024]{0:T(1024)(128)(2,1)S(1)}, bf16[1024,2048]{1,0:T(8,128)(2,1)}, ...), branch_computations={%region_11.11_spmd, %region_12.14_spmd} | conditional | flops 1360790656 | bytes 13130256 | solution.py:164
  443.9 2.8 fusion.117
  448.0 7.3 %fusion.29 = f32[128,1024]{1,0:T(8,128)S(1)} fusion(bf16[2048,1024]{1,0:T(8,128)(2,1)} %get-tuple-element.436, bf16[1024,2048]{1,0:T(8,128)(2,1)} %get-tuple-element.434, f32[2048]{0:T(1024)S(1)} %get-tuple-element.435, f32[128,1024]{1,0:T(8,128)} %get-tuple-element.704, f32[1024]{0:T(1024)S(1)} %convert_element_type.116, f32[128]{0:T(128)S(1)} %add_rsqrt_fusion.1, ...), kind=kOutput, calls=%fused_computation.50 | convolution fusion | flops 1091567616 | bytes 9450496 | tf_op jit(solution)/shard_map/while/body/eval_jaxpr/cond/branch_1_fun/dot_general | solution.py:158
  456.5 11.5 %reduce-scatter.2.cloned.1.call-done = bf16[128,512]{1,0:T(8,128)(2,1)} async-done(((bf16[128,1024]{1,0:T(8,128)(2,1)}), bf16[128,512]{1,0:T(8,128)(2,1)}) %reduce-scatter.2.cloned.1.call-update) | async-done | bytes 131088 | tf_op jit(solution)/shard_map/while/body/eval_jaxpr/reduce_scatter | solution.py:165
  469.1 1.9 fusion.128
  471.1 6.5 %all_gather.40 = bf16[4,32,1024]{2,1,0:T(8,128)(2,1)S(1)} all-gather(bf16[4,32,512]{2,1,0:T(8,128)(2,1)S(1)} %get-tuple-element.728), channel_id=1, replica_groups=mesh['dp'=8,'section'=2,'tensor'=2] {'tensor'}, dimensions={2}, use_global_device_ids=true | all-gather | bytes 393216 | tf_op jit(solution)/shard_map/while/body/eval_jaxpr/all_gather | solution.py:117
  478.7 5.6 all_gather.41
  486.4 26.6 %reduce-scatter.2.cloned.1.call-done = bf16[128,512]{1,0:T(8,128)(2,1)} async-done(((bf16[128,1024]{1,0:T(8,128)(2,1)}), bf16[128,512]{1,0:T(8,128)(2,1)}) %reduce-scatter.2.cloned.1.call-update) | async-done | bytes 131088 | tf_op jit(solution)/shard_map/while/body/eval_jaxpr/reduce_scatter | solution.py:165
  516.1 6.5 %all_gather.40 = bf16[4,32,1024]{2,1,0:T(8,128)(2,1)S(1)} all-gather(bf16[4,32,512]{2,1,0:T(8,128)(2,1)S(1)} %get-tuple-element.728), channel_id=1, replica_groups=mesh['dp'=8,'section'=2,'tensor'=2] {'tensor'}, dimensions={2}, use_global_device_ids=true | all-gather | bytes 393216 | tf_op jit(solution)/shard_map/while/body/eval_jaxpr/all_gather | solution.py:117
  523.7 5.7 all_gather.41
  531.5 11.4 %reduce-scatter.2.cloned.1.call-done = bf16[128,512]{1,0:T(8,128)(2,1)} async-done(((bf16[128,1024]{1,0:T(8,128)(2,1)}), bf16[128,512]{1,0:T(8,128)(2,1)}) %reduce-scatter.2.cloned.1.call-update) | async-done | bytes 131088 | tf_op jit(solution)/shard_map/while/body/eval_jaxpr/reduce_scatter | solution.py:165
  547.9 20.0 %all-reduce.2.cloned.1.call-done = bf16[16,32,512]{2,1,0:T(8,128)(2,1)} async-done(((bf16[16,32,512]{2,1,0:T(8,128)(2,1)}), bf16[16,32,512]{2,1,0:T(8,128)(2,1)}) %all-reduce.2.cloned.1.call-update) | async-done | bytes 524304 | tf_op jit(solution)/shard_map/psum | solution.py:18
  (206 shorter events, 62.5 us)
Async XLA Ops:
  6.5 5.1 copy-start
  6.5 66.6 %all-gather.7.cloned.1.call-start = ((), (), s32[]{:S(2)}) async-start(), calls=%async_computation.3 | async-start | bytes 2359296 | tf_op jit(solution)/shard_map/all_gather | solution.py:101
  7.3 129.1 %all-gather.5.cloned.1.call-start = ((), (), s32[]{:S(2)}) async-start(), calls=%async_computation.2 | async-start | bytes 3538944 | tf_op jit(solution)/shard_map/all_gather | solution.py:100
  9.3 200.3 %all-gather.9.cloned.1.call-start = ((), (), s32[]{:S(2)}) async-start(), calls=%async_computation.4 | async-start | bytes 4718592 | tf_op jit(solution)/shard_map/all_gather | solution.py:102
  10.0 274.6 %all-gather.11.cloned.1.call-start = ((), (), s32[]{:S(2)}) async-start(), calls=%async_computation.5 | async-start | bytes 4718592 | tf_op jit(solution)/shard_map/all_gather | solution.py:103
  11.6 9.7 %copy-start.6 = (s32[128]{0:T(128)S(1)}, s32[128]{0:T(128)}, u32[]{:S(2)}) copy-start(s32[128]{0:T(128)} %param.19) | copy-start | bytes 1540
  11.7 9.8 %copy-start.5 = (s32[128]{0:T(128)S(1)}, s32[128]{0:T(128)}, u32[]{:S(2)}) copy-start(s32[128]{0:T(128)} %param.18) | copy-start | bytes 1540
  11.7 10.1 %copy-start.2 = (bf16[1,2048]{1,0:T(2,128)(2,1)S(1)}, bf16[1,2048]{1,0:T(2,128)(2,1)}, u32[]{:S(2)}) copy-start(bf16[1,2048]{1,0:T(2,128)(2,1)} %param.23) | copy-start | bytes 12292
  11.7 10.1 %copy-start.3 = (bf16[1,1024]{1,0:T(2,128)(2,1)S(1)}, bf16[1,1024]{1,0:T(2,128)(2,1)}, u32[]{:S(2)}) copy-start(bf16[1,1024]{1,0:T(2,128)(2,1)} %param.25) | copy-start | bytes 6148
  11.7 10.1 %copy-start.4 = (bf16[1,1024]{1,0:T(2,128)(2,1)S(1)}, bf16[1,1024]{1,0:T(2,128)(2,1)}, u32[]{:S(2)}) copy-start(bf16[1,1024]{1,0:T(2,128)(2,1)} %param.26) | copy-start | bytes 6148
  14.1 44.5 %all-to-all-start = ((bf16[16,32,1024]{2,1,0:T(8,128)(2,1)}), bf16[16,32,1024]{2,1,0:T(8,128)(2,1)S(1)}, u32[]{:S(2)}, u32[]{:S(2)}) async-start(bf16[16,32,1024]{2,1,0:T(8,128)(2,1)} %copy.29), calls=%async_computation.1 | async-start | bytes 2097152 | tf_op jit(solution)/shard_map/all_to_all | solution.py:88
  21.4 264.4 %copy-start.1 = (bf16[1024]{0:T(1024)(128)(2,1)S(1)}, bf16[1024]{0:T(1024)(128)(2,1)}, u32[]{:S(2)}) copy-start(bf16[1024]{0:T(1024)(128)(2,1)} %param.27) | copy-start | bytes 6148
  285.8 41.4 %reduce-scatter.2.cloned.1.call-start = ((), (), s32[]{:S(2)}) async-start(), calls=%async_computation.7 | async-start | bytes 393216 | tf_op jit(solution)/shard_map/while/body/eval_jaxpr/reduce_scatter | solution.py:165
  328.2 2.0 collective-permute-start
  330.3 43.9 %reduce-scatter.2.cloned.1.call-start = ((), (), s32[]{:S(2)}) async-start(), calls=%async_computation.7 | async-start | bytes 393216 | tf_op jit(solution)/shard_map/while/body/eval_jaxpr/reduce_scatter | solution.py:165
  375.2 2.0 collective-permute-start
  377.2 43.9 %reduce-scatter.2.cloned.1.call-start = ((), (), s32[]{:S(2)}) async-start(), calls=%async_computation.7 | async-start | bytes 393216 | tf_op jit(solution)/shard_map/while/body/eval_jaxpr/reduce_scatter | solution.py:165
  422.1 2.0 collective-permute-start
  424.1 43.9 %reduce-scatter.2.cloned.1.call-start = ((), (), s32[]{:S(2)}) async-start(), calls=%async_computation.7 | async-start | bytes 393216 | tf_op jit(solution)/shard_map/while/body/eval_jaxpr/reduce_scatter | solution.py:165
  469.0 2.0 collective-permute-start
  471.1 41.9 %reduce-scatter.2.cloned.1.call-start = ((), (), s32[]{:S(2)}) async-start(), calls=%async_computation.7 | async-start | bytes 393216 | tf_op jit(solution)/shard_map/while/body/eval_jaxpr/reduce_scatter | solution.py:165
  514.1 2.0 collective-permute-start
  516.1 26.8 %reduce-scatter.2.cloned.1.call-start = ((), (), s32[]{:S(2)}) async-start(), calls=%async_computation.7 | async-start | bytes 393216 | tf_op jit(solution)/shard_map/while/body/eval_jaxpr/reduce_scatter | solution.py:165
  544.0 2.0 collective-permute-start
  546.0 21.9 %all-reduce.2.cloned.1.call-start = ((), (), s32[]{:S(2)}) async-start(), calls=%async_computation.6 | async-start | bytes 1048576 | tf_op jit(solution)/shard_map/psum | solution.py:18
Sparse Core Ops, SparseCore 0:
  9.5 63.6 all-gather.6
  75.2 61.1 all-gather.4
  138.5 70.9 all-gather.8
  211.4 73.1 all-gather.10
  316.9 10.2 reduce-scatter.1
  362.3 11.7 reduce-scatter.1
  409.2 11.7 reduce-scatter.1
  456.2 11.7 reduce-scatter.1
  486.1 26.8 reduce-scatter.1
  531.1 11.7 reduce-scatter.1
  549.1 18.7 all-reduce.1
where the time goes:
time: 577 us; the launch traced here: 576 us
  waiting for transfers between devices  365 us (63%)
  blocking collectives  72.4 us (13%)
  matrix products  64.4 us (11%)
  other arithmetic  41.1 us (7%)
  between operations  13.2 us (2%)
  local copies, waits for them, and re-layouts  11.3 us (2%)
  starting transfers between devices  7.91 us (1%)
    reduce_scatter x6, waiting for transfers between devices, advance(): lax.psum_scatter(partial_value.astype(jnp.bfloat16), 'tensor', scatter_di...  82.3 us
    all_gather x1, waiting for transfers between devices, local(): lax.all_gather(down_weight, 'dp', axis=2, tiled=True)  75.1 us
    all_gather x1, waiting for transfers between devices, local(): lax.all_gather(up_weight, 'dp', axis=1, tiled=True)  73.2 us
    all_gather x1, waiting for transfers between devices, local(): lax.all_gather(qkv_weight, 'dp', axis=1, tiled=True)  63.3 us
    all_gather x6, blocking collectives, advance(): current = lax.all_gather(carried, 'tensor', axis=2, tiled=True)  38.3 us
    all_to_all x1, waiting for transfers between devices, local(): lax.all_to_all(outgoing, 'dp', split_axis=0, concat_axis=0, tiled=True)  36.7 us
    all_gather x6, blocking collectives, advance(): joined = lax.all_gather(head_out, 'tensor', axis=2, tiled=True)  34 us
    dot_general x4, matrix products, mlp_part(): jnp.dot(hidden, down_full, preferred_element_type=jnp.float32)  29.2 us
  transfers between devices with their start and end apart: 18, of which 12 were waited for; matrix products, arithmetic and copies ran while one was open for 4% of the time, Pallas kernels for 0%

commit v1 on v0

--- a/solution.py
+++ b/solution.py
@@ -6,6 +6,17 @@
 MICRO = 4
 HEAD_DIM = 64
 epsilon = 1e-06
+
+
+def gather_around(x, axis, dim):
+    ways = lax.axis_size(axis)
+    pieces = [x]
+    for far in range(1, ways):
+        pieces.append(
+            lax.ppermute(pieces[far - 1], axis, [(d, (d - 1) % ways) for d in range(ways)])
+        )
+    line = jnp.concatenate(pieces, axis=dim)
+    return jnp.roll(line, lax.axis_index(axis) * x.shape[dim], axis=dim)
 
 
 def passed_along(value, axis, by):
@@ -97,7 +108,7 @@
     arrived_batches = arrived.reshape(batch_count, batch_images, block_rows, model_width)
     live_batches = live_counts.reshape(batch_count, batch_images)
     qkv_full, out_full, up_full, down_full = (
-        lax.all_gather(qkv_weight, "dp", axis=1, tiled=True),
+        gather_around(qkv_weight, "dp", 1),
         lax.all_gather(out_weight, "dp", axis=1, tiled=True),
         lax.all_gather(up_weight, "dp", axis=1, tiled=True),
         lax.all_gather(down_weight, "dp", axis=2, tiled=True),

time: 577 us -> 558 us (0.967)
  waiting for transfers between devices: 365 us -> 285 us
  starting transfers between devices: 7.91 us -> 41.5 us
  local copies, waits for them, and re-layouts: 11.3 us -> 37.3 us
    ppermute x0 -> x7, waiting for transfers between devices: none -> 71.8 us  [gather_around(): lax.ppermute(pieces[far - 1], axis, [(d, (d - 1) % ways) for d in range(w...]
    all_gather x1 -> x0, waiting for transfers between devices: 63.3 us -> none  [local(): lax.all_gather(qkv_weight, 'dp', axis=1, tiled=True)]
    all_gather x1, waiting for transfers between devices: 73.2 us -> 34.2 us  [local(): lax.all_gather(up_weight, 'dp', axis=1, tiled=True)]
    ppermute x0 -> x7, starting transfers between devices: none -> 37.4 us  [gather_around(): lax.ppermute(pieces[far - 1], axis, [(d, (d - 1) % ways) for d in range(w...]
    all_to_all x1, waiting for transfers between devices: 36.7 us -> 0.01 us  [local(): lax.all_to_all(outgoing, 'dp', split_axis=0, concat_axis=0, tiled=True)]
    unnamed x16 -> x35, local copies, waits for them, and re-layouts: 3.53 us -> 23.7 us
    all_gather x1, waiting for transfers between devices: 12.2 us -> 0.01 us  [local(): lax.all_gather(out_weight, 'dp', axis=1, tiled=True)]
  transfers between devices with their start and end apart: 18 -> 24, of which waited for: 12 -> 16; matrix products, arithmetic and copies ran while one was open for 4% -> 9% of each run, Pallas kernels for 0% -> 0%
where the time goes in v1:
time: 558 us; the launch traced here: 557 us
  waiting for transfers between devices  285 us (51%)
  blocking collectives  72.4 us (13%)
  matrix products  64.5 us (12%)
  starting transfers between devices  41.5 us (7%)
  other arithmetic  40.9 us (7%)
  local copies, waits for them, and re-layouts  37.3 us (7%)
  between operations  13.6 us (2%)
    reduce_scatter x6, waiting for transfers between devices, advance(): lax.psum_scatter(partial_value.astype(jnp.bfloat16), 'tensor', scatter_di...  82.3 us
    all_gather x1, waiting for transfers between devices, local(): lax.all_gather(down_weight, 'dp', axis=2, tiled=True)  75.3 us
    ppermute x7, waiting for transfers between devices, gather_around(): lax.ppermute(pieces[far - 1], axis, [(d, (d - 1) % ways) for d in range(w...  71.8 us
    all_gather x6, blocking collectives, advance(): current = lax.all_gather(carried, 'tensor', axis=2, tiled=True)  38.3 us
    ppermute x7, starting transfers between devices, gather_around(): lax.ppermute(pieces[far - 1], axis, [(d, (d - 1) % ways) for d in range(w...  37.4 us
    all_gather x1, waiting for transfers between devices, local(): lax.all_gather(up_weight, 'dp', axis=1, tiled=True)  34.2 us
    all_gather x6, blocking collectives, advance(): joined = lax.all_gather(head_out, 'tensor', axis=2, tiled=True)  34 us
    dot_general x4, matrix products, mlp_part(): jnp.dot(hidden, down_full, preferred_element_type=jnp.float32)  29.2 us
  transfers between devices with their start and end apart: 24, of which 16 were waited for; matrix products, arithmetic and copies ran while one was open for 9% of the time, Pallas kernels for 0%

profile of v1, /device:TPU:0, one launch (start us, length us, event | category | flops | bytes accessed | tf_op | source)
XLA Modules:
  0.0 556.6 jit_solution(9524280476235672162)
XLA Ops:
  10.0 6.1 %collective-permute-start.1 = (bf16[1,128,3,512]{1,3,2,0:T(8,128)(2,1)S(1)}, bf16[1,128,3,512]{1,3,2,0:T(8,128)(2,1)S(1)}, u32[]{:S(2)}, u32[]{:S(2)}) collective-permute-start(bf16[1,128,3,512]{1,3,2,0:T(8,128)(2,1)S(1)} %copy.38), channel_id=1, source_target_pairs={{0,28},{4,0},{8,4},{12,8},{16,12},{20,16},{24,20},{28,24},{1,29},{... | collective-permute-start | bytes 1179656 | tf_op jit(solution)/shard_map/ppermute | solution.py:16
  17.1 12.0 %collective-permute-done.1 = bf16[1,128,3,512]{1,3,2,0:T(8,128)(2,1)S(1)} collective-permute-done((bf16[1,128,3,512]{1,3,2,0:T(8,128)(2,1)S(1)}, bf16[1,128,3,512]{1,3,2,0:T(8,128)(2,1)S(1)}, u32[]{:S(2)}, u32[]{:S(2)}) %collective-permute-start.1) | collective-permute-done | bytes 393248 | tf_op jit(solution)/shard_map/ppermute | solution.py:16
  29.1 5.2 collective-permute-start.2
  43.8 5.2 collective-permute-start.3
  49.0 34.4 %collective-permute-done.3 = bf16[1,128,3,512]{1,3,2,0:T(8,128)(2,1)S(1)} collective-permute-done((bf16[1,128,3,512]{1,3,2,0:T(8,128)(2,1)S(1)}, bf16[1,128,3,512]{1,3,2,0:T(8,128)(2,1)S(1)}, u32[]{:S(2)}, u32[]{:S(2)}) %collective-permute-start.3) | collective-permute-done | bytes 393248 | tf_op jit(solution)/shard_map/ppermute | solution.py:16
  84.2 5.2 collective-permute-start.4
  89.4 5.3 collective-permute-done.4
  94.7 5.3 collective-permute-start.5
  101.3 5.6 %collective-permute-done.5 = bf16[1,128,3,512]{1,3,2,0:T(8,128)(2,1)} collective-permute-done((bf16[1,128,3,512]{1,3,2,0:T(8,128)(2,1)}, bf16[1,128,3,512]{1,3,2,0:T(8,128)(2,1)}, u32[]{:S(2)}, u32[]{:S(2)}) %collective-permute-start.5) | collective-permute-done | bytes 393248 | tf_op jit(solution)/shard_map/ppermute | solution.py:16
  106.9 5.2 collective-permute-start.6
  120.1 5.2 collective-permute-start.7
  131.3 8.1 %collective-permute-done.7 = bf16[1,128,3,512]{1,3,2,0:T(8,128)(2,1)} collective-permute-done((bf16[1,128,3,512]{1,3,2,0:T(8,128)(2,1)}, bf16[1,128,3,512]{1,3,2,0:T(8,128)(2,1)}, u32[]{:S(2)}, u32[]{:S(2)}) %collective-permute-start.7) | collective-permute-done | bytes 393248 | tf_op jit(solution)/shard_map/ppermute | solution.py:16
  151.8 3.8 constant_dynamic-slice_fusion.1
  155.7 34.2 %all-gather.6.cloned.1.call-done = bf16[1,1024,2048]{2,1,0:T(8,128)(2,1)} async-done(((bf16[1,128,2048]{2,1,0:T(8,128)(2,1)}), bf16[1,1024,2048]{2,1,0:T(8,128)(2,1)}) %all-gather.6.cloned.1.call-update) | async-done | bytes 4194320 | tf_op jit(solution)/shard_map/all_gather | solution.py:113
  189.9 75.3 %all-gather.8.cloned.1.call-done = bf16[1,2048,1024]{2,1,0:T(8,128)(2,1)} async-done(((bf16[1,2048,128]{2,1,0:T(8,128)(2,1)}), bf16[1,2048,1024]{2,1,0:T(8,128)(2,1)}) %all-gather.8.cloned.1.call-update) | async-done | bytes 4194320 | tf_op jit(solution)/shard_map/all_gather | solution.py:114
  266.3 260.2 %while.18 = (s32[]{:T(128)}, bf16[4,32,512]{2,1,0:T(8,128)(2,1)S(1)}, bf16[4,4,32,1024]{3,2,1,0:T(8,128)(2,1)}, s32[]{:T(128)}, pred[]{:T(512)}, /*index=5*/bf16...) while((s32[]{:T(128)}, ...), condition=%wide.region_18.19_spmd.clone, body=%wide.region_4.18_spmd.clone.sunk | while | flops 1817675392 | bytes 26838016 | solution.py:190
  266.4 5.6 %all_gather.36 = bf16[4,32,1024]{2,1,0:T(8,128)(2,1)S(1)} all-gather(bf16[4,32,512]{2,1,0:T(8,128)(2,1)S(1)} %get-tuple-element.728), channel_id=1, replica_groups=mesh['dp'=8,'section'=2,'tensor'=2] {'tensor'}, dimensions={2}, use_global_device_ids=true | all-gather | bytes 393216 | tf_op jit(solution)/shard_map/while/body/eval_jaxpr/all_gather | solution.py:128
  273.0 6.5 %conditional.6 = (bf16[4,32,512]{2,1,0:T(8,128)(2,1)S(1)}) conditional(s32[]{:T(128)} %convert_element_type.220, () %tuple.73, (bf16[4,32,1024]{2,1,0:T(8,128)(2,1)S(1)}, bf16[1024]{0:T(1024)(128)(2,1)S(1)}, bf16[1,1024,3,512]{1,3,2,0:T(8,128)(2,1)}, s32[]{:T(128)}, s32[4,4]{1,0:T(4,128)S(1)}) %tuple.74), branch_computations={%region_5.5_spmd, %region_6.10_spmd} | conditional | flops 454720768 | bytes 7793876 | solution.py:157
  279.5 5.6 %all_gather.37 = bf16[4,32,1024]{2,1,0:T(8,128)(2,1)S(1)} all-gather(bf16[4,32,512]{2,1,0:T(8,128)(2,1)S(1)} %get-tuple-element.769), channel_id=1, replica_groups=mesh['dp'=8,'section'=2,'tensor'=2] {'tensor'}, dimensions={2}, use_global_device_ids=true | all-gather | bytes 393216 | tf_op jit(solution)/shard_map/while/body/eval_jaxpr/all_gather | solution.py:158
  285.1 11.4 %conditional.7 = (f32[128,1024]{1,0:T(8,128)}, f32[128,1024]{1,0:T(8,128)S(1)}) conditional(s32[]{:T(128)} %convert_element_type.220, () %tuple.72, (bf16[4,32,1024]{2,1,0:T(8,128)(2,1)S(1)}, bf16[4,32,1024]{2,1,0:T(8,128)(2,1)S(1)}, bf16[1024,1024]{1,0:T(8,128)(2,1)}, bf16[1024]{0:T(1024)(128)(2,1)S(1)}, bf16[1024,2048]{1,0:T(8,128)(2,1)}, ...), branch_computations={%region_11.11_spmd, %region_12.14_spmd} | conditional | flops 1360790656 | bytes 13130256 | solution.py:175
  289.2 7.3 %fusion.29 = f32[128,1024]{1,0:T(8,128)S(1)} fusion(bf16[2048,1024]{1,0:T(8,128)(2,1)} %get-tuple-element.436, bf16[1024,2048]{1,0:T(8,128)(2,1)} %get-tuple-element.434, f32[2048]{0:T(1024)S(1)} %get-tuple-element.435, f32[128,1024]{1,0:T(8,128)} %get-tuple-element.704, f32[1024]{0:T(1024)S(1)} %convert_element_type.116, f32[128]{0:T(128)S(1)} %add_rsqrt_fusion.1, ...), kind=kOutput, calls=%fused_computation.50 | convolution fusion | flops 1091567616 | bytes 9450496 | tf_op jit(solution)/shard_map/while/body/eval_jaxpr/cond/branch_1_fun/dot_general | solution.py:169
  297.8 9.9 %reduce-scatter.2.cloned.1.call-done = bf16[128,512]{1,0:T(8,128)(2,1)} async-done(((bf16[128,1024]{1,0:T(8,128)(2,1)}), bf16[128,512]{1,0:T(8,128)(2,1)}) %reduce-scatter.2.cloned.1.call-update) | async-done | bytes 131088 | tf_op jit(solution)/shard_map/while/body/eval_jaxpr/reduce_scatter | solution.py:176
  310.8 6.5 %all_gather.36 = bf16[4,32,1024]{2,1,0:T(8,128)(2,1)S(1)} all-gather(bf16[4,32,512]{2,1,0:T(8,128)(2,1)S(1)} %get-tuple-element.728), channel_id=1, replica_groups=mesh['dp'=8,'section'=2,'tensor'=2] {'tensor'}, dimensions={2}, use_global_device_ids=true | all-gather | bytes 393216 | tf_op jit(solution)/shard_map/while/body/eval_jaxpr/all_gather | solution.py:128
  318.3 6.5 %conditional.6 = (bf16[4,32,512]{2,1,0:T(8,128)(2,1)S(1)}) conditional(s32[]{:T(128)} %convert_element_type.220, () %tuple.73, (bf16[4,32,1024]{2,1,0:T(8,128)(2,1)S(1)}, bf16[1024]{0:T(1024)(128)(2,1)S(1)}, bf16[1,1024,3,512]{1,3,2,0:T(8,128)(2,1)}, s32[]{:T(128)}, s32[4,4]{1,0:T(4,128)S(1)}) %tuple.74), branch_computations={%region_5.5_spmd, %region_6.10_spmd} | conditional | flops 454720768 | bytes 7793876 | solution.py:157
  324.8 5.7 %all_gather.37 = bf16[4,32,1024]{2,1,0:T(8,128)(2,1)S(1)} all-gather(bf16[4,32,512]{2,1,0:T(8,128)(2,1)S(1)} %get-tuple-element.769), channel_id=1, replica_groups=mesh['dp'=8,'section'=2,'tensor'=2] {'tensor'}, dimensions={2}, use_global_device_ids=true | all-gather | bytes 393216 | tf_op jit(solution)/shard_map/while/body/eval_jaxpr/all_gather | solution.py:158
  330.5 11.4 %conditional.7 = (f32[128,1024]{1,0:T(8,128)}, f32[128,1024]{1,0:T(8,128)S(1)}) conditional(s32[]{:T(128)} %convert_element_type.220, () %tuple.72, (bf16[4,32,1024]{2,1,0:T(8,128)(2,1)S(1)}, bf16[4,32,1024]{2,1,0:T(8,128)(2,1)S(1)}, bf16[1024,1024]{1,0:T(8,128)(2,1)}, bf16[1024]{0:T(1024)(128)(2,1)S(1)}, bf16[1024,2048]{1,0:T(8,128)(2,1)}, ...), branch_computations={%region_11.11_spmd, %region_12.14_spmd} | conditional | flops 1360790656 | bytes 13130256 | solution.py:175
  334.7 7.3 %fusion.29 = f32[128,1024]{1,0:T(8,128)S(1)} fusion(bf16[2048,1024]{1,0:T(8,128)(2,1)} %get-tuple-element.436, bf16[1024,2048]{1,0:T(8,128)(2,1)} %get-tuple-element.434, f32[2048]{0:T(1024)S(1)} %get-tuple-element.435, f32[128,1024]{1,0:T(8,128)} %get-tuple-element.704, f32[1024]{0:T(1024)S(1)} %convert_element_type.116, f32[128]{0:T(128)S(1)} %add_rsqrt_fusion.1, ...), kind=kOutput, calls=%fused_computation.50 | convolution fusion | flops 1091567616 | bytes 9450496 | tf_op jit(solution)/shard_map/while/body/eval_jaxpr/cond/branch_1_fun/dot_general | solution.py:169
  343.2 11.5 %reduce-scatter.2.cloned.1.call-done = bf16[128,512]{1,0:T(8,128)(2,1)} async-done(((bf16[128,1024]{1,0:T(8,128)(2,1)}), bf16[128,512]{1,0:T(8,128)(2,1)}) %reduce-scatter.2.cloned.1.call-update) | async-done | bytes 131088 | tf_op jit(solution)/shard_map/while/body/eval_jaxpr/reduce_scatter | solution.py:176
  357.7 6.5 %all_gather.36 = bf16[4,32,1024]{2,1,0:T(8,128)(2,1)S(1)} all-gather(bf16[4,32,512]{2,1,0:T(8,128)(2,1)S(1)} %get-tuple-element.728), channel_id=1, replica_groups=mesh['dp'=8,'section'=2,'tensor'=2] {'tensor'}, dimensions={2}, use_global_device_ids=true | all-gather | bytes 393216 | tf_op jit(solution)/shard_map/while/body/eval_jaxpr/all_gather | solution.py:128
  365.3 6.5 %conditional.6 = (bf16[4,32,512]{2,1,0:T(8,128)(2,1)S(1)}) conditional(s32[]{:T(128)} %convert_element_type.220, () %tuple.73, (bf16[4,32,1024]{2,1,0:T(8,128)(2,1)S(1)}, bf16[1024]{0:T(1024)(128)(2,1)S(1)}, bf16[1,1024,3,512]{1,3,2,0:T(8,128)(2,1)}, s32[]{:T(128)}, s32[4,4]{1,0:T(4,128)S(1)}) %tuple.74), branch_computations={%region_5.5_spmd, %region_6.10_spmd} | conditional | flops 454720768 | bytes 7793876 | solution.py:157
  365.6 3.6 fusion.12
  371.8 5.7 %all_gather.37 = bf16[4,32,1024]{2,1,0:T(8,128)(2,1)S(1)} all-gather(bf16[4,32,512]{2,1,0:T(8,128)(2,1)S(1)} %get-tuple-element.769), channel_id=1, replica_groups=mesh['dp'=8,'section'=2,'tensor'=2] {'tensor'}, dimensions={2}, use_global_device_ids=true | all-gather | bytes 393216 | tf_op jit(solution)/shard_map/while/body/eval_jaxpr/all_gather | solution.py:158
  377.5 11.4 %conditional.7 = (f32[128,1024]{1,0:T(8,128)}, f32[128,1024]{1,0:T(8,128)S(1)}) conditional(s32[]{:T(128)} %convert_element_type.220, () %tuple.72, (bf16[4,32,1024]{2,1,0:T(8,128)(2,1)S(1)}, bf16[4,32,1024]{2,1,0:T(8,128)(2,1)S(1)}, bf16[1024,1024]{1,0:T(8,128)(2,1)}, bf16[1024]{0:T(1024)(128)(2,1)S(1)}, bf16[1024,2048]{1,0:T(8,128)(2,1)}, ...), branch_computations={%region_11.11_spmd, %region_12.14_spmd} | conditional | flops 1360790656 | bytes 13130256 | solution.py:175
  381.6 7.3 %fusion.29 = f32[128,1024]{1,0:T(8,128)S(1)} fusion(bf16[2048,1024]{1,0:T(8,128)(2,1)} %get-tuple-element.436, bf16[1024,2048]{1,0:T(8,128)(2,1)} %get-tuple-element.434, f32[2048]{0:T(1024)S(1)} %get-tuple-element.435, f32[128,1024]{1,0:T(8,128)} %get-tuple-element.704, f32[1024]{0:T(1024)S(1)} %convert_element_type.116, f32[128]{0:T(128)S(1)} %add_rsqrt_fusion.1, ...), kind=kOutput, calls=%fused_computation.50 | convolution fusion | flops 1091567616 | bytes 9450496 | tf_op jit(solution)/shard_map/while/body/eval_jaxpr/cond/branch_1_fun/dot_general | solution.py:169
  390.1 11.5 %reduce-scatter.2.cloned.1.call-done = bf16[128,512]{1,0:T(8,128)(2,1)} async-done(((bf16[128,1024]{1,0:T(8,128)(2,1)}), bf16[128,512]{1,0:T(8,128)(2,1)}) %reduce-scatter.2.cloned.1.call-update) | async-done | bytes 131088 | tf_op jit(solution)/shard_map/while/body/eval_jaxpr/reduce_scatter | solution.py:176
  404.6 6.5 %all_gather.36 = bf16[4,32,1024]{2,1,0:T(8,128)(2,1)S(1)} all-gather(bf16[4,32,512]{2,1,0:T(8,128)(2,1)S(1)} %get-tuple-element.728), channel_id=1, replica_groups=mesh['dp'=8,'section'=2,'tensor'=2] {'tensor'}, dimensions={2}, use_global_device_ids=true | all-gather | bytes 393216 | tf_op jit(solution)/shard_map/while/body/eval_jaxpr/all_gather | solution.py:128
  412.2 6.5 %conditional.6 = (bf16[4,32,512]{2,1,0:T(8,128)(2,1)S(1)}) conditional(s32[]{:T(128)} %convert_element_type.220, () %tuple.73, (bf16[4,32,1024]{2,1,0:T(8,128)(2,1)S(1)}, bf16[1024]{0:T(1024)(128)(2,1)S(1)}, bf16[1,1024,3,512]{1,3,2,0:T(8,128)(2,1)}, s32[]{:T(128)}, s32[4,4]{1,0:T(4,128)S(1)}) %tuple.74), branch_computations={%region_5.5_spmd, %region_6.10_spmd} | conditional | flops 454720768 | bytes 7793876 | solution.py:157
  418.7 5.7 %all_gather.37 = bf16[4,32,1024]{2,1,0:T(8,128)(2,1)S(1)} all-gather(bf16[4,32,512]{2,1,0:T(8,128)(2,1)S(1)} %get-tuple-element.769), channel_id=1, replica_groups=mesh['dp'=8,'section'=2,'tensor'=2] {'tensor'}, dimensions={2}, use_global_device_ids=true | all-gather | bytes 393216 | tf_op jit(solution)/shard_map/while/body/eval_jaxpr/all_gather | solution.py:158
  424.4 11.4 %conditional.7 = (f32[128,1024]{1,0:T(8,128)}, f32[128,1024]{1,0:T(8,128)S(1)}) conditional(s32[]{:T(128)} %convert_element_type.220, () %tuple.72, (bf16[4,32,1024]{2,1,0:T(8,128)(2,1)S(1)}, bf16[4,32,1024]{2,1,0:T(8,128)(2,1)S(1)}, bf16[1024,1024]{1,0:T(8,128)(2,1)}, bf16[1024]{0:T(1024)(128)(2,1)S(1)}, bf16[1024,2048]{1,0:T(8,128)(2,1)}, ...), branch_computations={%region_11.11_spmd, %region_12.14_spmd} | conditional | flops 1360790656 | bytes 13130256 | solution.py:175
  428.5 7.3 %fusion.29 = f32[128,1024]{1,0:T(8,128)S(1)} fusion(bf16[2048,1024]{1,0:T(8,128)(2,1)} %get-tuple-element.436, bf16[1024,2048]{1,0:T(8,128)(2,1)} %get-tuple-element.434, f32[2048]{0:T(1024)S(1)} %get-tuple-element.435, f32[128,1024]{1,0:T(8,128)} %get-tuple-element.704, f32[1024]{0:T(1024)S(1)} %convert_element_type.116, f32[128]{0:T(128)S(1)} %add_rsqrt_fusion.1, ...), kind=kOutput, calls=%fused_computation.50 | convolution fusion | flops 1091567616 | bytes 9450496 | tf_op jit(solution)/shard_map/while/body/eval_jaxpr/cond/branch_1_fun/dot_general | solution.py:169
  437.0 11.5 %reduce-scatter.2.cloned.1.call-done = bf16[128,512]{1,0:T(8,128)(2,1)} async-done(((bf16[128,1024]{1,0:T(8,128)(2,1)}), bf16[128,512]{1,0:T(8,128)(2,1)}) %reduce-scatter.2.cloned.1.call-update) | async-done | bytes 131088 | tf_op jit(solution)/shard_map/while/body/eval_jaxpr/reduce_scatter | solution.py:176
  451.6 6.5 %all_gather.36 = bf16[4,32,1024]{2,1,0:T(8,128)(2,1)S(1)} all-gather(bf16[4,32,512]{2,1,0:T(8,128)(2,1)S(1)} %get-tuple-element.728), channel_id=1, replica_groups=mesh['dp'=8,'section'=2,'tensor'=2] {'tensor'}, dimensions={2}, use_global_device_ids=true | all-gather | bytes 393216 | tf_op jit(solution)/shard_map/while/body/eval_jaxpr/all_gather | solution.py:128
  459.1 5.6 %all_gather.37 = bf16[4,32,1024]{2,1,0:T(8,128)(2,1)S(1)} all-gather(bf16[4,32,512]{2,1,0:T(8,128)(2,1)S(1)} %get-tuple-element.769), channel_id=1, replica_groups=mesh['dp'=8,'section'=2,'tensor'=2] {'tensor'}, dimensions={2}, use_global_device_ids=true | all-gather | bytes 393216 | tf_op jit(solution)/shard_map/while/body/eval_jaxpr/all_gather | solution.py:158
  466.9 26.6 %reduce-scatter.2.cloned.1.call-done = bf16[128,512]{1,0:T(8,128)(2,1)} async-done(((bf16[128,1024]{1,0:T(8,128)(2,1)}), bf16[128,512]{1,0:T(8,128)(2,1)}) %reduce-scatter.2.cloned.1.call-update) | async-done | bytes 131088 | tf_op jit(solution)/shard_map/while/body/eval_jaxpr/reduce_scatter | solution.py:176
  496.6 6.5 %all_gather.36 = bf16[4,32,1024]{2,1,0:T(8,128)(2,1)S(1)} all-gather(bf16[4,32,512]{2,1,0:T(8,128)(2,1)S(1)} %get-tuple-element.728), channel_id=1, replica_groups=mesh['dp'=8,'section'=2,'tensor'=2] {'tensor'}, dimensions={2}, use_global_device_ids=true | all-gather | bytes 393216 | tf_op jit(solution)/shard_map/while/body/eval_jaxpr/all_gather | solution.py:128
  504.1 5.7 %all_gather.37 = bf16[4,32,1024]{2,1,0:T(8,128)(2,1)S(1)} all-gather(bf16[4,32,512]{2,1,0:T(8,128)(2,1)S(1)} %get-tuple-element.769), channel_id=1, replica_groups=mesh['dp'=8,'section'=2,'tensor'=2] {'tensor'}, dimensions={2}, use_global_device_ids=true | all-gather | bytes 393216 | tf_op jit(solution)/shard_map/while/body/eval_jaxpr/all_gather | solution.py:158
  512.0 11.5 %reduce-scatter.2.cloned.1.call-done = bf16[128,512]{1,0:T(8,128)(2,1)} async-done(((bf16[128,1024]{1,0:T(8,128)(2,1)}), bf16[128,512]{1,0:T(8,128)(2,1)}) %reduce-scatter.2.cloned.1.call-update) | async-done | bytes 131088 | tf_op jit(solution)/shard_map/while/body/eval_jaxpr/reduce_scatter | solution.py:176
  528.5 19.6 %all-reduce.2.cloned.1.call-done = bf16[16,32,512]{2,1,0:T(8,128)(2,1)} async-done(((bf16[16,32,512]{2,1,0:T(8,128)(2,1)}), bf16[16,32,512]{2,1,0:T(8,128)(2,1)}) %all-reduce.2.cloned.1.call-update) | async-done | bytes 524304 | tf_op jit(solution)/shard_map/psum | solution.py:29
  (238 shorter events, 120.7 us)
Async XLA Ops:
  6.5 27.8 %copy-start = (bf16[16,32,1024]{2,1,0:T(8,128)(2,1)S(1)}, bf16[16,32,1024]{2,1,0:T(8,128)(2,1)}, u32[]{:S(2)}) copy-start(bf16[16,32,1024]{2,1,0:T(8,128)(2,1)} %param.17) | copy-start | bytes 3145732
  6.5 93.5 %copy-start.8 = (s32[128]{0:T(128)S(1)}, s32[128]{0:T(128)}, u32[]{:S(2)}) copy-start(s32[128]{0:T(128)} %param.19) | copy-start | bytes 1540
  6.5 93.6 %copy-start.7 = (s32[128]{0:T(128)S(1)}, s32[128]{0:T(128)}, u32[]{:S(2)}) copy-start(s32[128]{0:T(128)} %param.18) | copy-start | bytes 1540
  6.5 93.9 %copy-start.4 = (bf16[1,2048]{1,0:T(2,128)(2,1)S(1)}, bf16[1,2048]{1,0:T(2,128)(2,1)}, u32[]{:S(2)}) copy-start(bf16[1,2048]{1,0:T(2,128)(2,1)} %param.23) | copy-start | bytes 12292
  6.5 93.9 %copy-start.5 = (bf16[1,1024]{1,0:T(2,128)(2,1)S(1)}, bf16[1,1024]{1,0:T(2,128)(2,1)}, u32[]{:S(2)}) copy-start(bf16[1,1024]{1,0:T(2,128)(2,1)} %param.25) | copy-start | bytes 6148
  6.5 93.9 %copy-start.6 = (bf16[1,1024]{1,0:T(2,128)(2,1)S(1)}, bf16[1,1024]{1,0:T(2,128)(2,1)}, u32[]{:S(2)}) copy-start(bf16[1,1024]{1,0:T(2,128)(2,1)} %param.26) | copy-start | bytes 6148
  6.6 149.1 %all-gather.4.cloned.1.call-start = ((), (), s32[]{:S(2)}) async-start(), calls=%async_computation.2 | async-start | bytes 2359296 | tf_op jit(solution)/shard_map/all_gather | solution.py:112
  7.3 182.6 %all-gather.6.cloned.1.call-start = ((), (), s32[]{:S(2)}) async-start(), calls=%async_computation.3 | async-start | bytes 4718592 | tf_op jit(solution)/shard_map/all_gather | solution.py:113
  8.0 257.1 %all-gather.8.cloned.1.call-start = ((), (), s32[]{:S(2)}) async-start(), calls=%async_computation.4 | async-start | bytes 4718592 | tf_op jit(solution)/shard_map/all_gather | solution.py:114
  10.0 19.1 %collective-permute-start.1 = (bf16[1,128,3,512]{1,3,2,0:T(8,128)(2,1)S(1)}, bf16[1,128,3,512]{1,3,2,0:T(8,128)(2,1)S(1)}, u32[]{:S(2)}, u32[]{:S(2)}) collective-permute-start(bf16[1,128,3,512]{1,3,2,0:T(8,128)(2,1)S(1)} %copy.38), channel_id=1, source_target_pairs={{0,28},{4,0},{8,4},{12,8},{16,12},{20,16},{24,20},{28,24},{1,29},{... | collective-permute-start | bytes 1179656 | tf_op jit(solution)/shard_map/ppermute | solution.py:16
  29.1 14.7 %collective-permute-start.2 = (bf16[1,128,3,512]{1,3,2,0:T(8,128)(2,1)S(1)}, bf16[1,128,3,512]{1,3,2,0:T(8,128)(2,1)S(1)}, u32[]{:S(2)}, u32[]{:S(2)}) collective-permute-start(bf16[1,128,3,512]{1,3,2,0:T(8,128)(2,1)S(1)} %collective-permute-done.1), channel_id=1, source_target_pairs={{0,28},{4,0},{8,4},{12,8},{16,12},{20,16},{24,20},{28,24},{1,29},{... | collective-permute-start | bytes 1179656 | tf_op jit(solution)/shard_map/ppermute | solution.py:16
  36.7 88.6 %all-to-all-start = ((bf16[16,32,1024]{2,1,0:T(8,128)(2,1)}), bf16[16,32,1024]{2,1,0:T(8,128)(2,1)S(1)}, u32[]{:S(2)}, u32[]{:S(2)}) async-start(bf16[16,32,1024]{2,1,0:T(8,128)(2,1)} %copy.35), calls=%async_computation.1 | async-start | bytes 2097152 | tf_op jit(solution)/shard_map/all_to_all | solution.py:99
  43.8 39.6 %collective-permute-start.3 = (bf16[1,128,3,512]{1,3,2,0:T(8,128)(2,1)S(1)}, bf16[1,128,3,512]{1,3,2,0:T(8,128)(2,1)S(1)}, u32[]{:S(2)}, u32[]{:S(2)}) collective-permute-start(bf16[1,128,3,512]{1,3,2,0:T(8,128)(2,1)S(1)} %collective-permute-done.2), channel_id=1, source_target_pairs={{0,28},{4,0},{8,4},{12,8},{16,12},{20,16},{24,20},{28,24},{1,29},{... | collective-permute-start | bytes 1179656 | tf_op jit(solution)/shard_map/ppermute | solution.py:16
  83.4 0.7 copy-start.1
  84.2 10.5 %collective-permute-start.4 = (bf16[1,128,3,512]{1,3,2,0:T(8,128)(2,1)S(1)}, bf16[1,128,3,512]{1,3,2,0:T(8,128)(2,1)}, u32[]{:S(2)}, u32[]{:S(2)}) collective-permute-start(bf16[1,128,3,512]{1,3,2,0:T(8,128)(2,1)S(1)} %collective-permute-done.3), channel_id=1, source_target_pairs={{0,28},{4,0},{8,4},{12,8},{16,12},{20,16},{24,20},{28,24},{1,29},{... | collective-permute-start | bytes 1179656 | tf_op jit(solution)/shard_map/ppermute | solution.py:16
  94.7 12.2 %collective-permute-start.5 = (bf16[1,128,3,512]{1,3,2,0:T(8,128)(2,1)}, bf16[1,128,3,512]{1,3,2,0:T(8,128)(2,1)}, u32[]{:S(2)}, u32[]{:S(2)}) collective-permute-start(bf16[1,128,3,512]{1,3,2,0:T(8,128)(2,1)} %collective-permute-done.4), channel_id=1, source_target_pairs={{0,28},{4,0},{8,4},{12,8},{16,12},{20,16},{24,20},{28,24},{1,29},{... | collective-permute-start | bytes 1179656 | tf_op jit(solution)/shard_map/ppermute | solution.py:16
  106.9 13.2 %collective-permute-start.6 = (bf16[1,128,3,512]{1,3,2,0:T(8,128)(2,1)}, bf16[1,128,3,512]{1,3,2,0:T(8,128)(2,1)}, u32[]{:S(2)}, u32[]{:S(2)}) collective-permute-start(bf16[1,128,3,512]{1,3,2,0:T(8,128)(2,1)} %collective-permute-done.5), channel_id=1, source_target_pairs={{0,28},{4,0},{8,4},{12,8},{16,12},{20,16},{24,20},{28,24},{1,29},{... | collective-permute-start | bytes 1179656 | tf_op jit(solution)/shard_map/ppermute | solution.py:16
  120.1 19.3 %collective-permute-start.7 = (bf16[1,128,3,512]{1,3,2,0:T(8,128)(2,1)}, bf16[1,128,3,512]{1,3,2,0:T(8,128)(2,1)}, u32[]{:S(2)}, u32[]{:S(2)}) collective-permute-start(bf16[1,128,3,512]{1,3,2,0:T(8,128)(2,1)} %collective-permute-done.6), channel_id=1, source_target_pairs={{0,28},{4,0},{8,4},{12,8},{16,12},{20,16},{24,20},{28,24},{1,29},{... | collective-permute-start | bytes 1179656 | tf_op jit(solution)/shard_map/ppermute | solution.py:16
  125.3 18.4 %copy-start.2 = (bf16[1,128,3,512]{1,3,2,0:T(8,128)(2,1)S(1)}, bf16[1,128,3,512]{1,3,2,0:T(8,128)(2,1)}, u32[]{:S(2)}) copy-start(bf16[1,128,3,512]{1,3,2,0:T(8,128)(2,1)} %copy-done.1) | copy-start | bytes 1179652
  142.9 123.4 %copy-start.3 = (bf16[1024]{0:T(1024)(128)(2,1)S(1)}, bf16[1024]{0:T(1024)(128)(2,1)}, u32[]{:S(2)}) copy-start(bf16[1024]{0:T(1024)(128)(2,1)} %param.27) | copy-start | bytes 6148
  266.3 41.4 %reduce-scatter.2.cloned.1.call-start = ((), (), s32[]{:S(2)}) async-start(), calls=%async_computation.6 | async-start | bytes 393216 | tf_op jit(solution)/shard_map/while/body/eval_jaxpr/reduce_scatter | solution.py:176
  308.8 2.0 collective-permute-start
  310.8 43.9 %reduce-scatter.2.cloned.1.call-start = ((), (), s32[]{:S(2)}) async-start(), calls=%async_computation.6 | async-start | bytes 393216 | tf_op jit(solution)/shard_map/while/body/eval_jaxpr/reduce_scatter | solution.py:176
  355.7 2.0 collective-permute-start
  357.7 43.9 %reduce-scatter.2.cloned.1.call-start = ((), (), s32[]{:S(2)}) async-start(), calls=%async_computation.6 | async-start | bytes 393216 | tf_op jit(solution)/shard_map/while/body/eval_jaxpr/reduce_scatter | solution.py:176
  402.6 2.0 collective-permute-start
  404.6 43.9 %reduce-scatter.2.cloned.1.call-start = ((), (), s32[]{:S(2)}) async-start(), calls=%async_computation.6 | async-start | bytes 393216 | tf_op jit(solution)/shard_map/while/body/eval_jaxpr/reduce_scatter | solution.py:176
  449.6 2.0 collective-permute-start
  451.6 41.9 %reduce-scatter.2.cloned.1.call-start = ((), (), s32[]{:S(2)}) async-start(), calls=%async_computation.6 | async-start | bytes 393216 | tf_op jit(solution)/shard_map/while/body/eval_jaxpr/reduce_scatter | solution.py:176
  494.5 2.0 collective-permute-start
  496.6 26.9 %reduce-scatter.2.cloned.1.call-start = ((), (), s32[]{:S(2)}) async-start(), calls=%async_computation.6 | async-start | bytes 393216 | tf_op jit(solution)/shard_map/while/body/eval_jaxpr/reduce_scatter | solution.py:176
  524.5 2.0 collective-permute-start
  526.5 21.6 %all-reduce.2.cloned.1.call-start = ((), (), s32[]{:S(2)}) async-start(), calls=%async_computation.5 | async-start | bytes 1048576 | tf_op jit(solution)/shard_map/psum | solution.py:29
Sparse Core Ops, SparseCore 0:
  9.5 74.4 all-gather.3
  86.1 103.7 all-gather.5
  192.0 73.1 all-gather.7
  297.4 10.2 reduce-scatter.1
  342.9 11.7 reduce-scatter.1
  389.8 11.7 reduce-scatter.1
  436.7 11.7 reduce-scatter.1
  466.6 26.8 reduce-scatter.1
  511.6 11.7 reduce-scatter.1
  529.3 18.7 all-reduce.1
